TPU v7x, 512 devices: a whole 4x4x16 slice. The times are simulated.
512 devices in a mesh: quarter: 4 (over x), row: 8 (over z_lo), col: 16 (over y, z_hi, core).
Axes of the slice: x: 4, y: 4, z: 16 (z_hi: 2, z_lo: 8; z = z_hi * 8 + z_lo), core: 2. Of those that a mesh axis runs over, the one named last changes fastest.
Arguments:
- grad: bfloat16 [4, 4096, 4096], P('quarter', 'row', 'col'), may hold values from -6 to 6
- left_root: bfloat16 [4096, 4096], P('row', 'col'), may hold values from -1 to 3, as said below
- right_root: bfloat16 [4, 4096, 4096], P('quarter', 'row', 'col'), may hold values from -1 to 3, as said below
- momentum: float32 [4, 4096, 4096], P('quarter', 'row', 'col'), may hold values from -6 to 6
- weights: bfloat16 [4, 4096, 4096], P('quarter', 'row', 'col'), may hold values from -6 to 6
Outputs:
- momentum_new: float32 [4, 4096, 4096], P('quarter', 'row', 'col')
- new_weights: bfloat16 [4, 4096, 4096], P(None, ('row', 'quarter'), 'col')
Inputs may be any that keep to these rules, and one draw needn't show every extreme that they name: `left_root`: symmetric. `right_root`: each block symmetric.
All inputs are finite; a program needn't handle non-finite values.
Results may differ from a plain program's by a relative error of at most 0.001.
Values may be sent and summed in bfloat16 or wider, within the bound.
No kernel may reach another device: no remote copies, remote signals or barrier semaphores. Data moves between devices by JAX's collectives and lax.ppermute only.
A program may use at most 64 MiB of HBM per device.

v0:
```python
import jax
import jax.numpy as jnp
from jax import lax
from jax.sharding import PartitionSpec as P

decay_rate = 0.9
step_rate = 0.1


def per_device(grad, left_root, right_root, momentum, weights):
    right_panel = lax.all_gather(right_root, "row", axis=1, tiled=True)[0]
    mixed = jnp.dot(
        lax.all_gather(grad, "col", axis=2, tiled=True)[0],
        right_panel,
        preferred_element_type=jnp.float32,
    ).astype(jnp.bfloat16)
    left_panel = lax.all_gather(left_root, "col", axis=1, tiled=True)
    product = jnp.dot(
        left_panel,
        lax.all_gather(mixed, "row", axis=0, tiled=True),
        preferred_element_type=jnp.float32,
    )
    renewed = decay_rate * momentum[0] + (1.0 - decay_rate) * product
    updated = (weights[0].astype(jnp.float32) - step_rate * renewed).astype(jnp.bfloat16)
    spread = lax.all_to_all(updated[None], "quarter", split_axis=1, concat_axis=0, tiled=True)
    return (renewed[None], spread)


def solution(mesh):
    placed = (
        P("quarter", "row", "col"),
        P("row", "col"),
        P("quarter", "row", "col"),
        P("quarter", "row", "col"),
        P("quarter", "row", "col"),
    )
    return jax.shard_map(
        per_device,
        mesh=mesh,
        in_specs=placed,
        out_specs=(P("quarter", "row", "col"), P(None, ("row", "quarter"), "col")),
        check_vma=False,
    )
```

profile of v0, /device:TPU:8, one launch (start us, length us, event | category | flops | bytes accessed | tf_op | source)
XLA Modules:
  0.0 411.7 jit_solution(7492663751729316780)
XLA Ops:
  7.2 0.0 all-gather.7.cloned.1.call-start
  7.2 0.7 all-gather.7.cloned.1.call-update
  7.9 0.0 all-gather.5.cloned.1.call-start
  7.9 0.7 all-gather.5.cloned.1.call-update
  8.6 0.0 copy-start
  8.7 0.0 all-gather.11.cloned.1.call-start
  8.7 0.7 all-gather.11.cloned.1.call-update
  9.4 0.0 copy-start.1
  9.4 0.0 all-gather.9.cloned.1.call-start
  9.4 75.3 %all-gather.7.cloned.1.call-done = bf16[1,4096,256]{2,1,0:T(8,128)(2,1)} async-done(((bf16[1,512,256]{2,1,0:T(8,128)(2,1)}), bf16[1,4096,256]{2,1,0:T(8,128)(2,1)}) %all-gather.7.cloned.1.call-update) | async-done | bytes 2097168 | tf_op jit(solution)/shard_map/all_gather | solution.py:11
  84.7 116.1 %all-gather.5.cloned.1.call-done = bf16[1,512,4096]{2,1,0:T(8,128)(2,1)} async-done(((bf16[1,512,256]{2,1,0:T(8,128)(2,1)}), bf16[1,512,4096]{2,1,0:T(8,128)(2,1)}) %all-gather.5.cloned.1.call-update) | async-done | bytes 4194320 | tf_op jit(solution)/shard_map/all_gather | solution.py:13
  200.9 4.8 %fusion.5 = bf16[512,256]{1,0:T(8,128)(2,1)} fusion(bf16[1,4096,256]{2,1,0:T(8,128)(2,1)} %all-gather.7.cloned.1.call-done, bf16[1,512,4096]{2,1,0:T(8,128)(2,1)} %all-gather.5.cloned.1.call-done), kind=kOutput, calls=%fused_computation.6 | convolution fusion | flops 1073872896 | bytes 6553600 | tf_op jit(solution)/shard_map/dot_general | solution.py:12
  205.7 0.0 all-gather.9.cloned.1.call-update
  205.7 0.0 copy-done
  205.7 0.2 copy.15
  205.9 0.0 copy-done.1
  205.9 0.1 copy.16
  206.1 110.5 %all-gather.11.cloned.1.call-done = bf16[512,4096]{1,0:T(8,128)(2,1)} async-done(((bf16[512,256]{1,0:T(8,128)(2,1)}), bf16[512,4096]{1,0:T(8,128)(2,1)}) %all-gather.11.cloned.1.call-update) | async-done | bytes 4194320 | tf_op jit(solution)/shard_map/all_gather | solution.py:17
  316.6 68.4 %all-gather.9.cloned.1.call-done = bf16[4096,256]{1,0:T(8,128)(2,1)} async-done(((bf16[512,256]{1,0:T(8,128)(2,1)}), bf16[4096,256]{1,0:T(8,128)(2,1)}) %all-gather.9.cloned.1.call-update) | async-done | bytes 2097168 | tf_op jit(solution)/shard_map/all_gather | solution.py:20
  385.1 4.1 %fusion.4 = f32[512,256]{0,1:T(8,128)S(1)} fusion(bf16[4096,256]{1,0:T(8,128)(2,1)} %all-gather.9.cloned.1.call-done, bf16[512,4096]{1,0:T(8,128)(2,1)} %all-gather.11.cloned.1.call-done, f32[1,512,256]{1,2,0:T(8,128)S(1)} %copy.15), kind=kOutput, calls=%fused_computation.5 | convolution fusion | flops 1074135040 | bytes 7340032 | tf_op jit(solution)/shard_map/dot_general | solution.py:18
  389.2 0.1 fusion.11
  389.3 0.4 copy.17
  389.7 0.5 broadcast.13
  390.2 2.2 reduce
  392.4 0.8 reshape.12
  393.2 4.2 %all-to-all-start = ((bf16[4,2,16384]{2,1,0:T(2,128)(2,1)}), bf16[4,2,16384]{2,1,0:T(2,128)(2,1)S(1)}, u32[]{:S(2)}, u32[]{:S(2)}) async-start(bf16[4,2,16384]{2,1,0:T(2,128)(2,1)} %reshape.12), calls=%async_computation | async-start | bytes 524288 | tf_op jit(solution)/shard_map/all_to_all | solution.py:25
  397.4 1.0 copy.18
  398.4 5.7 %all-to-all-done = bf16[4,2,16384]{2,1,0:T(2,128)(2,1)S(1)} async-done(((bf16[4,2,16384]{2,1,0:T(2,128)(2,1)}), bf16[4,2,16384]{2,1,0:T(2,128)(2,1)S(1)}, u32[]{:S(2)}, u32[]{:S(2)}) %all-to-all-start) | async-done | bytes 262176 | tf_op jit(solution)/shard_map/all_to_all | solution.py:25
  404.1 0.3 reshape.13
  404.4 0.7 copy.19
Async XLA Ops:
  7.2 77.6 %all-gather.7.cloned.1.call-start = ((), (), s32[]{:S(2)}) async-start(), calls=%async_computation.2 | async-start | bytes 2359296 | tf_op jit(solution)/shard_map/all_gather | solution.py:11
  7.9 193.0 %all-gather.5.cloned.1.call-start = ((), (), s32[]{:S(2)}) async-start(), calls=%async_computation.1 | async-start | bytes 4456448 | tf_op jit(solution)/shard_map/all_gather | solution.py:13
  8.6 197.1 %copy-start = (f32[1,512,256]{2,1,0:T(8,128)S(1)}, f32[1,512,256]{2,1,0:T(8,128)}, u32[]{:S(2)}) copy-start(f32[1,512,256]{2,1,0:T(8,128)} %param.8) | copy-start | bytes 1572868
  8.7 307.9 %all-gather.11.cloned.1.call-start = ((), (), s32[]{:S(2)}) async-start(), calls=%async_computation.4 | async-start | bytes 4456448 | tf_op jit(solution)/shard_map/all_gather | solution.py:17
  9.4 196.5 %copy-start.1 = (bf16[1,512,256]{2,1,0:T(8,128)(2,1)S(1)}, bf16[1,512,256]{2,1,0:T(8,128)(2,1)}, u32[]{:S(2)}) copy-start(bf16[1,512,256]{2,1,0:T(8,128)(2,1)} %param.9) | copy-start | bytes 786436
  9.4 375.6 %all-gather.9.cloned.1.call-start = ((), (), s32[]{:S(2)}) async-start(), calls=%async_computation.3 | async-start | bytes 2359296 | tf_op jit(solution)/shard_map/all_gather | solution.py:20
  393.2 10.9 %all-to-all-start = ((bf16[4,2,16384]{2,1,0:T(2,128)(2,1)}), bf16[4,2,16384]{2,1,0:T(2,128)(2,1)S(1)}, u32[]{:S(2)}, u32[]{:S(2)}) async-start(bf16[4,2,16384]{2,1,0:T(2,128)(2,1)} %reshape.12), calls=%async_computation | async-start | bytes 524288 | tf_op jit(solution)/shard_map/all_to_all | solution.py:25
Sparse Core Ops, SparseCore 0:
  10.1 74.6 all-gather.6
  87.8 112.9 all-gather.4
  204.0 112.5 all-gather.10
  319.1 65.8 all-gather.8
where the time goes:
time: 412 us
  waiting for transfers between devices  378 us (92%)
  between operations  13.9 us (3%)
  matrix products  8.94 us (2%)
  starting transfers between devices  4.4 us (1%)
    all_gather x1, waiting for transfers between devices, per_device(): lax.all_gather(grad, 'col', axis=2, tiled=True)[0]  116 us
    all_gather x1, waiting for transfers between devices, per_device(): left_panel = lax.all_gather(left_root, 'col', axis=1, tiled=True)  111 us
    all_gather x1, waiting for transfers between devices, per_device(): right_panel = lax.all_gather(right_root, 'row', axis=1, tiled=True)[0]  75.3 us
    all_gather x1, waiting for transfers between devices, per_device(): lax.all_gather(mixed, 'row', axis=0, tiled=True)  68.4 us
  transfers between devices with their start and end apart: 5, of which 5 were waited for; matrix products, arithmetic and copies ran while one was open for 1% of the time, Pallas kernels for 0%

commit v1 on v0

--- a/solution.py
+++ b/solution.py
@@ -7,8 +7,13 @@
 step_rate = 0.1
 
 
+def all_by_exchange(block, axis, dim):
+    sent = jnp.stack([block] * lax.axis_size(axis))
+    return jnp.concatenate(lax.all_to_all(sent, axis, 0, 0), axis=dim)
+
+
 def per_device(grad, left_root, right_root, momentum, weights):
-    right_panel = lax.all_gather(right_root, "row", axis=1, tiled=True)[0]
+    right_panel = all_by_exchange(right_root, "row", 1)[0]
     mixed = jnp.dot(
         lax.all_gather(grad, "col", axis=2, tiled=True)[0],
         right_panel,

time: 412 us -> 388 us (0.942)
  waiting for transfers between devices: 378 us -> 189 us
  blocking collectives: 0 us -> 165 us
    all_to_all x0 -> x1, blocking collectives: none -> 165 us  [all_by_exchange(): return jnp.concatenate(lax.all_to_all(sent, axis, 0, 0), axis=dim)]
    all_gather x1, waiting for transfers between devices: 116 us -> 0.01 us  [per_device(): lax.all_gather(grad, 'col', axis=2, tiled=True)[0]]
    all_gather x1 -> x0, waiting for transfers between devices: 75.3 us -> none  [per_device(): right_panel = lax.all_gather(right_root, 'row', axis=1, tiled=True)[0]]
  transfers between devices with their start and end apart: 5 -> 4, of which waited for: 5 -> 3; matrix products, arithmetic and copies ran while one was open for 1% -> 2% of each run, Pallas kernels for 0% -> 0%
where the time goes in v1:
time: 388 us
  waiting for transfers between devices  189 us (49%)
  blocking collectives  165 us (43%)
  between operations  13.8 us (4%)
  matrix products  8.34 us (2%)
  local copies, waits for them, and re-layouts  5.14 us (1%)
  starting transfers between devices  4.36 us (1%)
    all_to_all x1, blocking collectives, all_by_exchange(): return jnp.concatenate(lax.all_to_all(sent, axis, 0, 0), axis=dim)  165 us
    all_gather x1, waiting for transfers between devices, per_device(): left_panel = lax.all_gather(left_root, 'col', axis=1, tiled=True)  113 us
    all_gather x1, waiting for transfers between devices, per_device(): lax.all_gather(mixed, 'row', axis=0, tiled=True)  68.6 us
  transfers between devices with their start and end apart: 4, of which 3 were waited for; matrix products, arithmetic and copies ran while one was open for 2% of the time, Pallas kernels for 0%

profile of v1, /device:TPU:8, one launch (start us, length us, event | category | flops | bytes accessed | tf_op | source)
XLA Modules:
  0.0 387.5 jit_solution(6214542115759843097)
XLA Ops:
  7.2 0.0 all-gather.4.cloned.1.call-start
  7.2 0.7 all-gather.4.cloned.1.call-update
  7.9 0.0 all-gather.8.cloned.1.call-start
  7.9 0.7 all-gather.8.cloned.1.call-update
  8.6 0.0 all-gather.6.cloned.1.call-start
  8.7 1.1 stack.2
  9.8 164.6 %all_to_all.17 = bf16[8,1,512,256]{3,2,1,0:T(8,128)(2,1)S(1)} all-to-all(bf16[8,1,512,256]{3,2,1,0:T(8,128)(2,1)S(1)} %stack.2), channel_id=1, replica_groups=mesh['quarter'=4,'row'=8,'col'=16] {'row'}, dimensions={0} | all-to-all | bytes 4194304 | tf_op jit(solution)/shard_map/all_to_all | solution.py:12
  174.4 0.0 all-gather.4.cloned.1.call-done
  174.4 0.0 copy-start
  174.4 0.0 copy-start.1
  174.4 4.2 %fusion.4 = bf16[512,256]{1,0:T(8,128)(2,1)} fusion(bf16[4096,256]{1,0:T(8,128)(2,1)S(1)} %bitcast.26, bf16[1,512,4096]{2,1,0:T(8,128)(2,1)} %all-gather.4.cloned.1.call-done), kind=kOutput, calls=%fused_computation.5 | convolution fusion | flops 1073872896 | bytes 6553600 | tf_op jit(solution)/shard_map/dot_general | solution.py:17
  178.6 0.0 all-gather.6.cloned.1.call-update
  178.7 0.0 copy-done
  178.7 0.2 copy.15
  178.9 0.0 copy-done.1
  178.9 0.1 copy.16
  179.0 113.2 %all-gather.8.cloned.1.call-done = bf16[512,4096]{1,0:T(8,128)(2,1)} async-done(((bf16[512,256]{1,0:T(8,128)(2,1)}), bf16[512,4096]{1,0:T(8,128)(2,1)}) %all-gather.8.cloned.1.call-update) | async-done | bytes 4194320 | tf_op jit(solution)/shard_map/all_gather | solution.py:22
  292.3 68.6 %all-gather.6.cloned.1.call-done = bf16[4096,256]{1,0:T(8,128)(2,1)} async-done(((bf16[512,256]{1,0:T(8,128)(2,1)}), bf16[4096,256]{1,0:T(8,128)(2,1)}) %all-gather.6.cloned.1.call-update) | async-done | bytes 2097168 | tf_op jit(solution)/shard_map/all_gather | solution.py:25
  360.9 4.1 %fusion.3 = f32[512,256]{0,1:T(8,128)S(1)} fusion(bf16[4096,256]{1,0:T(8,128)(2,1)} %all-gather.6.cloned.1.call-done, bf16[512,4096]{1,0:T(8,128)(2,1)} %all-gather.8.cloned.1.call-done, f32[1,512,256]{1,2,0:T(8,128)S(1)} %copy.15), kind=kOutput, calls=%fused_computation.4 | convolution fusion | flops 1074135040 | bytes 7340032 | tf_op jit(solution)/shard_map/dot_general | solution.py:23
  365.0 0.1 fusion.8
  365.1 0.4 copy.17
  365.5 0.5 broadcast.16
  366.1 2.2 reduce
  368.3 0.8 reshape.15
  369.0 4.2 %all-to-all-start.1 = ((bf16[4,2,16384]{2,1,0:T(2,128)(2,1)}), bf16[4,2,16384]{2,1,0:T(2,128)(2,1)S(1)}, u32[]{:S(2)}, u32[]{:S(2)}) async-start(bf16[4,2,16384]{2,1,0:T(2,128)(2,1)} %reshape.15), calls=%async_computation.1 | async-start | bytes 524288 | tf_op jit(solution)/shard_map/all_to_all | solution.py:30
  373.3 1.0 copy.18
  374.3 5.7 %all-to-all-done.1 = bf16[4,2,16384]{2,1,0:T(2,128)(2,1)S(1)} async-done(((bf16[4,2,16384]{2,1,0:T(2,128)(2,1)}), bf16[4,2,16384]{2,1,0:T(2,128)(2,1)S(1)}, u32[]{:S(2)}, u32[]{:S(2)}) %all-to-all-start.1) | async-done | bytes 262176 | tf_op jit(solution)/shard_map/all_to_all | solution.py:30
  380.0 0.3 reshape.16
  380.2 0.7 copy.19
Async XLA Ops:
  7.2 167.3 %all-gather.4.cloned.1.call-start = ((), (), s32[]{:S(2)}) async-start(), calls=%async_computation.2 | async-start | bytes 4456448 | tf_op jit(solution)/shard_map/all_gather | solution.py:18
  7.9 284.4 %all-gather.8.cloned.1.call-start = ((), (), s32[]{:S(2)}) async-start(), calls=%async_computation.4 | async-start | bytes 4456448 | tf_op jit(solution)/shard_map/all_gather | solution.py:22
  8.6 352.2 %all-gather.6.cloned.1.call-start = ((), (), s32[]{:S(2)}) async-start(), calls=%async_computation.3 | async-start | bytes 2359296 | tf_op jit(solution)/shard_map/all_gather | solution.py:25
  174.4 4.2 %copy-start = (f32[1,512,256]{2,1,0:T(8,128)S(1)}, f32[1,512,256]{2,1,0:T(8,128)}, u32[]{:S(2)}) copy-start(f32[1,512,256]{2,1,0:T(8,128)} %param.8) | copy-start | bytes 1572868
  174.4 4.5 %copy-start.1 = (bf16[1,512,256]{2,1,0:T(8,128)(2,1)S(1)}, bf16[1,512,256]{2,1,0:T(8,128)(2,1)}, u32[]{:S(2)}) copy-start(bf16[1,512,256]{2,1,0:T(8,128)(2,1)} %param.9) | copy-start | bytes 786436
  369.0 10.9 %all-to-all-start.1 = ((bf16[4,2,16384]{2,1,0:T(2,128)(2,1)}), bf16[4,2,16384]{2,1,0:T(2,128)(2,1)S(1)}, u32[]{:S(2)}, u32[]{:S(2)}) async-start(bf16[4,2,16384]{2,1,0:T(2,128)(2,1)} %reshape.15), calls=%async_computation.1 | async-start | bytes 524288 | tf_op jit(solution)/shard_map/all_to_all | solution.py:30
Sparse Core Ops, SparseCore 0:
  11.1 121.5 all-gather.3
  135.8 156.3 all-gather.7
  294.9 65.8 all-gather.5
